TPU v7x, 128 devices: a whole 4x4x4 slice. The times are simulated.
128 devices in a mesh: cls: 4 (over y), rows: 32 (over z, x, core).
Axes of the slice: x: 4, y: 4, z: 4, core: 2. Of those that a mesh axis runs over, the one named last changes fastest.
Arguments:
- prior: bfloat16 [65536, 1000], P('rows', 'cls'), may hold values from -6 to 6
- blocks: bfloat16 [256, 24, 256, 256], P('rows'), may hold values from -0.078125 to 0.078125
- links: int32 [256, 24], P('rows'), may hold values from 0 to 39, as said below
- counts: int32 [256], P('rows'), may hold values from 1 to 24
- fetch: int32 [32, 32, 1], P('rows'), may hold values from 0 to 7
- seeds: int32 [65536], P('rows'), may hold values from -1000 to 999
- inv_temp: float32 [65536], P('rows'), may hold values from 1 to 300
Outputs:
- pseudo: bfloat16 [65536, 1000], P('rows', 'cls')
- certainty: float32 [65536], P('rows')
Inputs may be any that keep to these rules, and one draw needn't show every extreme that they name: links index a slot list of 8 own tiles followed by one tile from each index of rows in order; every one of these slots is named by some link of its index of rows. `seeds`: a negative seed marks an image without a label.
All inputs are finite; a program needn't handle non-finite values.
Results may differ from a plain program's by a relative error of at most 0.0075.
The roundings to bfloat16 on the way count: a program that leaves them out, or rounds other values in their place, can miss the bound.
Values may be sent and summed in bfloat16 or wider, within the bound.
A program may use at most 192 MiB of HBM per device.

v0:
```python
import jax
import jax.numpy as jnp
from jax import lax
from jax.sharding import PartitionSpec as P

CLS = 1000


blend = 0.8


def propagate_local(column_set, blocks, slot_tiles, counts, targets):
    adjacent_blocks = column_set[slot_tiles]
    live_slots = jnp.arange(blocks.shape[1], dtype=jnp.int32)[None, :] < counts[:, None]
    adjacent_blocks = jnp.where(
        live_slots[:, :, None, None], adjacent_blocks, jnp.zeros((), jnp.bfloat16)
    )
    accumulated_sum = jnp.einsum(
        "mvfg,mvgx->mfx", blocks, adjacent_blocks, preferred_element_type=jnp.float32
    )
    return blend * accumulated_sum.reshape(targets.shape) + (1.0 - blend) * targets


def local(prior, blocks, links, counts, fetch, seeds, inv_temp):
    col_width = prior.shape[1]
    tile_rows = blocks.shape[2]
    own_tiles = blocks.shape[0]
    col_start = lax.axis_index("cls") * col_width
    targets = (
        seeds[:, None] == col_start + jnp.arange(col_width, dtype=jnp.int32)[None, :]
    ).astype(jnp.float32)
    wanted = lax.all_to_all(fetch, "rows", split_axis=1, concat_axis=0, tiled=True).reshape(-1)
    field = prior
    for rounds in range(2):
        tiled = field.reshape(own_tiles, tile_rows, col_width)
        outgoing = tiled[wanted].reshape(lax.axis_size("rows"), -1, tile_rows, col_width)
        arrived = lax.all_to_all(outgoing, "rows", split_axis=0, concat_axis=0, tiled=True)
        column_set = jnp.concatenate([tiled, arrived.reshape(-1, tile_rows, col_width)], axis=0)
        mixed = propagate_local(column_set, blocks, links, counts, targets)
        field = mixed.astype(jnp.bfloat16) if rounds == 0 else mixed
    logits = inv_temp[:, None] * field
    top = lax.pmax(jnp.max(logits, axis=1), "cls")
    shifted = logits - top[:, None]
    expo = jnp.exp(shifted)
    totals, moments = lax.psum((jnp.sum(expo, axis=1), jnp.sum(expo * shifted, axis=1)), "cls")
    pseudo = (expo / totals[:, None]).astype(jnp.bfloat16)
    certainty = 1.0 - (jnp.log(totals) - moments / totals) / jnp.log(jnp.float32(CLS))
    return (pseudo, certainty)


def solution(mesh):
    return jax.shard_map(
        local,
        mesh=mesh,
        in_specs=(
            P("rows", "cls"),
            P("rows", None, None, None),
            P("rows", None),
            P("rows"),
            P("rows", None, None),
            P("rows"),
            P("rows"),
        ),
        out_specs=(P("rows", "cls"), P("rows")),
        check_vma=False,
    )
```

profile of v0, /device:TPU:0, one launch (start us, length us, event | category | flops | bytes accessed | tf_op | source)
XLA Modules:
  0.0 283.6 jit_solution(14118641778013687975)
XLA Ops:
  0.6 0.7 copy.16
  1.4 15.4 %all_to_all.19 = s32[1,32,1]{2,0,1:T(1,128)S(1)} all-to-all(s32[1,32,1]{2,0,1:T(1,128)S(1)} %copy.16), channel_id=1, replica_groups=mesh['cls'=4,'rows'=32] {'rows'}, dimensions={1} | all-to-all | bytes 256 | tf_op jit(solution)/shard_map/all_to_all | solution.py:32
  16.8 0.7 reduce.3
  17.5 4.0 %gather_fusion = bf16[32,256,250]{2,1,0:T(8,128)(2,1)} fusion(bf16[8,256,250]{2,1,0:T(8,128)(2,1)} %bitcast.48, s32[1024]{0:T(1024)S(1)} %pad_clamp_fusion.1), kind=kCustom, calls=%fused_computation | custom fusion | bytes 8192128 | tf_op jit(solution)/shard_map/gather | solution.py:36
  21.5 0.0 copy-start.3
  21.5 0.0 copy-start.2
  21.5 0.0 copy-start.4
  21.5 0.0 copy-start
  21.5 5.0 %all-to-all-start.1 = ((bf16[32,1,256,250]{3,2,1,0:T(8,128)(2,1)}), bf16[32,1,256,250]{3,2,1,0:T(8,128)(2,1)}, u32[]{:S(2)}, u32[]{:S(2)}) async-start(bf16[32,1,256,250]{3,2,1,0:T(8,128)(2,1)} %bitcast.51), calls=%async_computation.1 | async-start | bytes 8388608 | tf_op jit(solution)/shard_map/all_to_all | solution.py:37
  26.5 0.0 copy-done.3
  26.5 0.1 reshape.165
  26.6 0.0 copy-done.2
  26.7 0.0 copy-done.4
  26.7 0.1 iota_compare_fusion
  26.7 53.7 %all-to-all-done.1 = bf16[32,1,256,250]{3,2,1,0:T(8,128)(2,1)} async-done(((bf16[32,1,256,250]{3,2,1,0:T(8,128)(2,1)}), bf16[32,1,256,250]{3,2,1,0:T(8,128)(2,1)}, u32[]{:S(2)}, u32[]{:S(2)}) %all-to-all-start.1) | async-done | bytes 4096032 | tf_op jit(solution)/shard_map/all_to_all | solution.py:37
  80.5 0.0 copy-done
  80.5 5.4 %pad_maximum_fusion = bf16[40,256,250]{2,1,0:T(8,128)(2,1)} fusion(bf16[32,256,250]{2,1,0:T(8,128)(2,1)} %bitcast.3, bf16[8,256,250]{2,1,0:T(8,128)(2,1)S(1)} %bitcast.49), kind=kLoop, calls=%fused_computation.12 | loop fusion | flops 2560000 | bytes 10240000 | tf_op jit(solution)/shard_map/concatenate | solution.py:38
  85.9 13.6 %gather_fusion.1 = bf16[192,256,250]{2,1,0:T(8,128)(2,1)} fusion(bf16[40,256,250]{2,1,0:T(8,128)(2,1)} %pad_maximum_fusion, s32[1024]{0:T(1024)S(1)} %pad_clamp_fusion), kind=kCustom, calls=%fused_computation.1 | custom fusion | bytes 49152768 | tf_op jit(solution)/shard_map/gather | solution.py:13
  99.5 32.5 %copy.17 = bf16[8,24,256,250]{2,3,1,0:T(8,128)(2,1)} copy(bf16[8,24,256,250]{3,2,1,0:T(8,128)(2,1)} %bitcast.47) | data formatting | bytes 49152000 | tf_op jit(solution)/shard_map/gather | solution.py:13
  132.0 18.3 %fusion.8 = bf16[8,256,250]{1,2,0:T(8,128)(2,1)S(1)} fusion(bf16[8,24,256,256]{3,2,1,0:T(8,128)(2,1)} %param.8, bf16[8,24,256,250]{2,3,1,0:T(8,128)(2,1)} %copy.17, pred[8,24]{1,0:T(8,128)(4,1)S(1)} %iota_compare_fusion, s32[8,256]{1,0:T(8,128)S(1)} %eq.25, s32[250]{0:T(256)S(1)} %iota_add_fusion), kind=kOutput, calls=%fused_computation.18 | convolution fusion | flops 6306304000 | bytes 50775208 | tf_op jit(solution)/shard_map/mvfg,mvgx->mfx/dot_general | solution.py:18
  150.4 2.8 gather_fusion.2
  153.2 0.0 copy-start.1
  153.2 5.0 %all-to-all-start.2 = ((bf16[32,1,256,250]{2,3,1,0:T(8,128)(2,1)}), bf16[32,1,256,250]{2,3,1,0:T(8,128)(2,1)}, u32[]{:S(2)}, u32[]{:S(2)}) async-start(bf16[32,1,256,250]{2,3,1,0:T(8,128)(2,1)} %bitcast.52), calls=%async_computation.2 | async-start | bytes 8388608 | tf_op jit(solution)/shard_map/all_to_all | solution.py:37
  158.1 0.0 copy-done.1
  158.2 53.9 %all-to-all-done.2 = bf16[32,1,256,250]{2,3,1,0:T(8,128)(2,1)} async-done(((bf16[32,1,256,250]{2,3,1,0:T(8,128)(2,1)}), bf16[32,1,256,250]{2,3,1,0:T(8,128)(2,1)}, u32[]{:S(2)}, u32[]{:S(2)}) %all-to-all-start.2) | async-done | bytes 4096032 | tf_op jit(solution)/shard_map/all_to_all | solution.py:37
  212.1 5.1 %pad_maximum_fusion.1 = bf16[40,256,250]{1,2,0:T(8,128)(2,1)} fusion(bf16[32,256,250]{1,2,0:T(8,128)(2,1)} %bitcast.10, bf16[8,256,250]{1,2,0:T(8,128)(2,1)S(1)} %fusion.8), kind=kLoop, calls=%fused_computation.13 | loop fusion | flops 2560000 | bytes 10240000 | tf_op jit(solution)/shard_map/concatenate | solution.py:38
  217.2 13.6 %gather_fusion.3 = bf16[192,256,250]{1,2,0:T(8,128)(2,1)} fusion(bf16[40,256,250]{1,2,0:T(8,128)(2,1)} %pad_maximum_fusion.1, s32[1024]{0:T(1024)S(1)} %pad_clamp_fusion), kind=kCustom, calls=%fused_computation.3 | custom fusion | bytes 49152768 | tf_op jit(solution)/shard_map/gather | solution.py:13
  230.7 19.8 %fusion.21 = (f32[8,256]{1,0:T(8,128)S(1)}, f32[8,256,250]{1,2,0:T(8,128)}) fusion(f32[8,256]{1,0:T(8,128)S(1)} %mul.60, s32[8,256]{1,0:T(8,128)S(1)} %eq.25, s32[250]{0:T(256)S(1)} %iota_add_fusion, bf16[8,24,256,256]{3,2,1,0:T(8,128)(2,1)} %param.8, bf16[8,24,256,250]{2,3,1,0:T(8,128)(2,1)} %bitcast.50, pred[8,24]{1,0:T(8,128)(4,1)S(1)} %iota_compare_fusion), kind=kOutput, calls=%fused_computation.30 | convolution fusion | flops 6306813952 | bytes 51815592 | tf_op jit(solution)/shard_map/mvfg,mvgx->mfx/dot_general | solution.py:18
  250.6 10.8 %pmax.7 = f32[2048]{0:T(1024)S(1)} all-reduce(f32[2048]{0:T(1024)S(1)} %bitcast.57), channel_id=1, replica_groups=mesh['cls'=4,'rows'=32] {'cls'}, use_global_device_ids=true, to_apply=%region_1.2 | all-reduce | flops 2048 | bytes 16384 | tf_op jit(solution)/shard_map/pmax | solution.py:42
  261.4 1.9 copy.19
  263.4 2.4 fusion.10
  265.8 14.3 %all-reduce = (f32[2048]{0:T(1024)S(1)}, f32[2048]{0:T(1024)S(1)}) all-reduce(f32[2048]{0:T(1024)S(1)} %bitcast.55, f32[2048]{0:T(1024)S(1)} %bitcast.56), channel_id=1, replica_groups=mesh['cls'=4,'rows'=32] {'cls'}, use_global_device_ids=true, to_apply=%region_3.4 | all-reduce | flops 4096 | bytes 32768 | tf_op jit(solution)/shard_map/psum | solution.py:45
  280.1 0.6 multiply_subtract_fusion
  280.7 2.9 %fusion.16 = bf16[2048,250]{1,0:T(8,128)(2,1)} fusion(f32[8,256,250]{2,1,0:T(8,128)S(1)} %copy.19, f32[2048]{0:T(1024)S(1)} %get-tuple-element.4, f32[2048]{0:T(1024)S(1)} %pmax.7, s32[250]{0:T(256)S(1)} %iota_add_fusion, f32[2048]{0:T(1024)S(1)} %copy-done.1, s32[2048]{0:T(1024)S(1)} %copy-done.2), kind=kLoop, calls=%fused_computation.29 | loop fusion | flops 3584000 | bytes 3105768 | tf_op jit(solution)/shard_map/convert_element_type | solution.py:46
  (11 shorter events, 0.1 us)
Async XLA Ops:
  21.5 5.0 %copy-start.3 = (s32[8,24]{1,0:T(8,128)S(1)}, s32[8,24]{1,0:T(8,128)}, u32[]{:S(2)}) copy-start(s32[8,24]{1,0:T(8,128)} %param.9) | copy-start | bytes 2308
  21.5 5.1 %copy-start.2 = (s32[2048]{0:T(1024)S(1)}, s32[2048]{0:T(1024)}, u32[]{:S(2)}) copy-start(s32[2048]{0:T(1024)} %param.12) | copy-start | bytes 24580
  21.5 5.2 %copy-start.4 = (s32[8]{0:T(128)S(1)}, s32[8]{0:T(128)}, u32[]{:S(2)}) copy-start(s32[8]{0:T(128)} %param.10) | copy-start | bytes 100
  21.5 59.0 %copy-start = (bf16[2048,250]{1,0:T(8,128)(2,1)S(1)}, bf16[2048,250]{1,0:T(8,128)(2,1)}, u32[]{:S(2)}) copy-start(bf16[2048,250]{1,0:T(8,128)(2,1)} %param.7) | copy-start | bytes 3072004
  21.5 59.0 %all-to-all-start.1 = ((bf16[32,1,256,250]{3,2,1,0:T(8,128)(2,1)}), bf16[32,1,256,250]{3,2,1,0:T(8,128)(2,1)}, u32[]{:S(2)}, u32[]{:S(2)}) async-start(bf16[32,1,256,250]{3,2,1,0:T(8,128)(2,1)} %bitcast.51), calls=%async_computation.1 | async-start | bytes 8388608 | tf_op jit(solution)/shard_map/all_to_all | solution.py:37
  153.2 5.0 %copy-start.1 = (f32[2048]{0:T(1024)S(1)}, f32[2048]{0:T(1024)}, u32[]{:S(2)}) copy-start(f32[2048]{0:T(1024)} %param.13) | copy-start | bytes 24580
  153.2 58.9 %all-to-all-start.2 = ((bf16[32,1,256,250]{2,3,1,0:T(8,128)(2,1)}), bf16[32,1,256,250]{2,3,1,0:T(8,128)(2,1)}, u32[]{:S(2)}, u32[]{:S(2)}) async-start(bf16[32,1,256,250]{2,3,1,0:T(8,128)(2,1)} %bitcast.52), calls=%async_computation.2 | async-start | bytes 8388608 | tf_op jit(solution)/shard_map/all_to_all | solution.py:37
where the time goes:
time: 285 us; the launch traced here: 284 us
  waiting for transfers between devices  108 us (38%)
  local copies, waits for them, and re-layouts  69.3 us (24%)
  blocking collectives  40.6 us (14%)
  matrix products  38.2 us (13%)
  other arithmetic  17.1 us (6%)
  starting transfers between devices  9.97 us (3%)
    all_to_all x2, waiting for transfers between devices, local(): lax.all_to_all(outgoing, 'rows', split_axis=0, concat_axis=0, tiled=True)  108 us
    gather x3, local copies, waits for them, and re-layouts, propagate_local(): adjacent_blocks = column_set[slot_tiles]  59.7 us
    dot_general x2, matrix products, propagate_local(): jnp.einsum('mvfg,mvgx->mfx', blocks, adjacent_blocks, preferred_element_t...  38.2 us
    all_to_all x1, blocking collectives, local(): lax.all_to_all(fetch, 'rows', split_axis=1, concat_axis=0, tiled=True)  15.4 us
    psum x1, blocking collectives, local(): lax.psum((jnp.sum(expo, axis=1), jnp.sum(expo * shifted, axis=1)), 'cls')  14.3 us
    pmax x1, blocking collectives, local(): top = lax.pmax(jnp.max(logits, axis=1), 'cls')  10.8 us
    concatenate x2, other arithmetic, local(): jnp.concatenate([tiled, arrived.reshape(-1, tile_rows, col_width)], axis=0)  10.5 us
    all_to_all x2, starting transfers between devices, local(): lax.all_to_all(outgoing, 'rows', split_axis=0, concat_axis=0, tiled=True)  9.97 us
  transfers between devices with their start and end apart: 2, of which 2 were waited for; matrix products, arithmetic and copies ran while one was open for 0% of the time, Pallas kernels for 0%

commit v1 on v0

v1 whole, which is shorter than its diff:
```python
import functools
import math

import jax
import jax.numpy as jnp
from jax import lax
from jax.experimental import pallas as pl
from jax.experimental.pallas import tpu as pltpu
from jax.sharding import PartitionSpec as P

CLS = 1000
NB = 24
TPD = 8
TILE = 256
W = 250
HALF = 128
Q = 64
ZERO = 40

BLEND = 0.8
MESH = pl.DeviceIdType.MESH

R1, R2, L1, L2, FR, FL, RR, RL, D0R, D1R, D0L, D1L, WR, WL, PT = range(15)

PEERS = [(0, dz, dc) for dz in range(4) for dc in range(2) if (dz, dc) != (0, 0)] + [
    (dx, 0, dc) for dx in range(1, 4) for dc in range(2)
]


def kernel(
    tab_a, tab_b, fetch_row, prior_hbm, blocks_hbm, seeds_ref, temp_ref,
    pseudo_hbm, cert_ref,
    *scratch,
):
    (pv, bv, acc, fld0, fld1, stage, frv, frm, seed_c, temp_c, stats, outv) = scratch[:12]
    gb = scratch[12:20]
    rl = scratch[20:28]
    cs = scratch[28:36]
    (send, recv, f_send, f_recv, y_send, y_recv, b_sem, loc) = scratch[36:]
    fld = (fld0, fld1)

    r = lax.axis_index("rows")
    y = lax.axis_index("cls")
    c = lax.rem(r, 2)
    x = lax.rem(r // 2, 4)
    z = r // 8

    def dev(dx, dz, dc):
        row = (lax.rem(z + dz, 4) * 4 + lax.rem(x + dx, 4)) * 2 + lax.rem(c + dc, 2)
        return (y, row)

    def idx(rnd, rt, kh):
        return (rnd * 2 + rt) * 2 + kh

    def step(rt, d, dc):
        return dev(0, d % 4, dc) if rt == 0 else dev(d % 4, 0, dc)

    def gstep(rt, d):
        return dev(d % 4, 0, 0) if rt == 0 else dev(0, d % 4, 0)

    prior_cp = pltpu.make_async_copy(prior_hbm, pv, loc.at[0])
    prior_cp.start()
    block_cps = [
        pltpu.make_async_copy(blocks_hbm.at[t], bv.at[t], b_sem.at[t]) for t in range(TPD)
    ]
    barrier = pltpu.get_barrier_semaphore()
    for p in PEERS:
        pl.semaphore_signal(barrier, inc=1, device_id=dev(*p), device_id_type=MESH)
    for dy in range(1, 4):
        pl.semaphore_signal(
            barrier, inc=1, device_id=(lax.rem(y + dy, 4), r), device_id_type=MESH
        )
    frv[0] = fetch_row[...]
    frv[8] = fetch_row[...]
    prior_cp.wait()
    for t in range(TPD):
        fld0[t, :, HALF:] = jnp.zeros((TILE, HALF), jnp.bfloat16)
        fld0[t, :, :W] = pv[t * TILE : (t + 1) * TILE, :]
    pl.semaphore_wait(barrier, len(PEERS) + 3)

    def g_copy(rnd, rt, kh, name):
        i = idx(rnd, rt, kh)
        lo, hi = slice(0, 4), slice(4, 8)
        rows = pl.ds(kh * HALF + rt * Q, Q)
        own = fld[rnd]
        src, dst, d = {
            R1: (own.at[lo, rows, :], gb[i].at[2, lo], 1),
            R2: (own.at[hi, rows, :], gb[i].at[2, hi], 1),
            L1: (own.at[hi, rows, :], gb[i].at[0, hi], -1),
            L2: (own.at[lo, rows, :], gb[i].at[0, lo], -1),
            FR: (gb[i].at[2, lo], gb[i].at[1, lo], 1),
            FL: (gb[i].at[0, hi], gb[i].at[1, hi], -1),
        }[name]
        return pltpu.make_async_remote_copy(
            src_ref=src, dst_ref=dst, send_sem=send.at[idx(0, rt, kh), name],
            recv_sem=recv.at[i, name], device_id=gstep(rt, d), device_id_type=MESH,
        )

    def p_copy(rnd, rt, kh, name):
        i = idx(rnd, rt, kh)
        s = idx(0, rt, kh)
        group = lambda g: stage.at[s, g]
        slot = lambda d, dc: cs[i].at[pl.ds((d * 2 + dc) * 4, 4)]
        src, dst, d, dc = {
            RR: (group(2), rl[i].at[0], 1, 0),
            RL: (group(3), rl[i].at[1], -1, 0),
            D0R: (group(0), slot(3, 0), 1, 0),
            D1R: (group(1), slot(3, 1), 1, 1),
            D0L: (group(4), slot(1, 0), -1, 0),
            D1L: (group(5), slot(1, 1), -1, 1),
            WR: (rl[i].at[0], slot(2, 0), 1, 0),
            WL: (rl[i].at[1], slot(2, 1), -1, 1),
            PT: (group(6), slot(0, 1), 0, 1),
        }[name]
        return pltpu.make_async_remote_copy(
            src_ref=src, dst_ref=dst, send_sem=send.at[s, name],
            recv_sem=recv.at[i, name], device_id=step(rt, d, dc), device_id_type=MESH,
        )

    def start_g(rnd, kh, names):
        for name in names:
            for rt in range(2):
                g_copy(rnd, rt, kh, name).start()

    def wait_g(rnd, kh, names):
        for name in names:
            for rt in range(2):
                g_copy(rnd, rt, kh, name).wait_recv()

    def start_p(rnd, kh, names):
        for name in names:
            for rt in range(2):
                p_copy(rnd, rt, kh, name).start()

    def wait_p(rnd, kh, names):
        for name in names:
            for rt in range(2):
                p_copy(rnd, rt, kh, name).wait_recv()

    def wait_sends(kh, rnd):
        for rt in range(2):
            for name in (R1, R2, L1, L2, FR, FL):
                g_copy(rnd, rt, kh, name).wait_send()
            for name in (RR, RL, D0R, D1R, D0L, D1L, WR, WL, PT):
                p_copy(rnd, rt, kh, name).wait_send()

    f_copies = []
    for k, (dx, dz, dc, base) in enumerate(
        [(0, dz, dc, 0) for dz in range(4) for dc in range(2) if (dz, dc) != (0, 0)]
        + [(dx, 0, dc, 8) for dx in range(4) for dc in range(2) if (dx, dc) != (0, 0)]
    ):
        d = dz if base == 0 else dx
        f_copies.append(
            pltpu.make_async_remote_copy(
                src_ref=fetch_row, dst_ref=frv.at[base + ((4 - d) % 4) * 2 + dc],
                send_sem=f_send.at[k], recv_sem=f_recv.at[k],
                device_id=dev(dx, dz, dc), device_id_type=MESH,
            )
        )

    def src_row(rt, d):
        if rt == 0:
            return (z * 4 + lax.rem(x + d, 4)) * 2 + c
        return (lax.rem(z + d, 4) * 4 + x) * 2 + c

    def select(rnd, kh):
        for rt in range(2):
            i = idx(rnd, rt, kh)
            rows = pl.ds(kh * HALF + rt * Q, Q)
            for d in range(4):
                row = src_row(rt, d)
                for dd in (2, 1, 3, 0):
                    for dc in range(2):
                        f = frm[rt * 8 + dd * 2 + dc, 0, row]
                        value = fld[rnd][f, rows, :] if d == 0 else gb[i][d - 1, f]
                        if (dd, dc) == (0, 0):
                            cs[i][d] = value
                        else:
                            g = 6 if dd == 0 else (dd - 1) * 2 + dc
                            stage[idx(0, rt, kh), g, d] = value

    def own_slots(rnd, t):
        for rt in range(2):
            for kh in range(2):
                a = kh * HALF + rt * Q
                cs[idx(rnd, rt, kh)][4 * TPD + t] = fld[rnd][t, a : a + Q, :]

    def product(rnd, kh, t):
        a = idx(rnd, 0, kh)
        b = idx(rnd, 1, kh)
        total = None
        for jp in range(NB // 2):
            left, right = [], []
            for j in (2 * jp, 2 * jp + 1):
                left.append(bv[t, j, :, kh * HALF : (kh + 1) * HALF])
                right.append(cs[a][tab_a[t * NB + j]])
                right.append(cs[b][tab_b[t * NB + j]])
            d = jnp.dot(
                jnp.concatenate(left, axis=1), jnp.concatenate(right, axis=0),
                preferred_element_type=jnp.float32,
            )
            total = d if total is None else total + d
        return total

    lane = lax.broadcasted_iota(jnp.int32, (TILE, TILE), 1)
    inside = lane < W
    column = lane + y * W

    def mixed(t, total):
        hit = (seed_c[t] == column) & inside
        return BLEND * total + jnp.where(hit, jnp.float32(1.0 - BLEND), jnp.float32(0.0))

    HOP1 = (R1, L1)
    HOP1B = (R2, L2)
    FWD = (FR, FL)
    SENDS = (RR, RL, D0R, D0L, D1R, D1L, PT)
    RELAY = (WR, WL)
    FINAL = (D0R, D0L, D1R, D1L, PT, WR, WL)

    start_g(0, 0, HOP1)
    for cp in f_copies:
        cp.start()
    start_g(0, 0, HOP1B)
    for cp in block_cps:
        cp.start()

    for rnd in range(2):
        for rt in range(2):
            for kh in range(2):
                cs[idx(rnd, rt, kh)][ZERO] = jnp.zeros((Q, TILE), jnp.bfloat16)
    for t in range(TPD):
        own_slots(0, t)
    seeds_t = jnp.transpose(seeds_ref[...].astype(jnp.float32), (1, 0))
    temps_t = jnp.transpose(temp_ref[...], (1, 0))
    for t in range(TPD):
        for h in range(2):
            k = 2 * t + h
            seed_c[t, h * HALF : (h + 1) * HALF, :] = seeds_t[:, k : k + 1].astype(jnp.int32)
            temp_c[t, h * HALF : (h + 1) * HALF, :] = temps_t[:, k : k + 1]
    for cp in f_copies:
        cp.wait()
    to_smem = pltpu.make_async_copy(frv, frm, loc.at[1])
    to_smem.start()
    to_smem.wait()

    def exchange(rnd):
        wait_g(rnd, 0, HOP1)
        start_g(rnd, 0, FWD)
        start_g(rnd, 1, HOP1 + HOP1B)
        wait_g(rnd, 0, HOP1B + FWD)
        select(rnd, 0)
        start_p(rnd, 0, SENDS)
        wait_g(rnd, 1, HOP1)
        start_g(rnd, 1, FWD)
        wait_p(rnd, 0, (RR, RL))
        start_p(rnd, 0, RELAY)
        wait_g(rnd, 1, HOP1B + FWD)
        select(rnd, 1)
        start_p(rnd, 1, SENDS)
        wait_p(rnd, 0, FINAL)

    def first_chunk(rnd):
        def body(t, carry):
            @pl.when(t == 4)
            def _():
                wait_p(rnd, 1, (RR, RL))
                start_p(rnd, 1, RELAY)

            acc[t] = product(rnd, 0, t)
            return carry

        lax.fori_loop(0, TPD, body, 0)
        wait_p(rnd, 1, FINAL)

    exchange(0)
    for cp in block_cps:
        cp.wait()
    first_chunk(0)
    for kh in range(2):
        wait_sends(kh, 0)

    def first_tile(t, carry):
        value = mixed(t, acc[t] + product(0, 1, t)).astype(jnp.bfloat16)
        fld1[t] = value
        for rt in range(2):
            for kh in range(2):
                a = kh * HALF + rt * Q
                cs[idx(1, rt, kh)][4 * TPD + t] = value[a : a + Q, :]

        @pl.when(t == 3)
        def _():
            start_g(1, 0, (R1, L2))

        return carry

    lax.fori_loop(0, TPD, first_tile, 0)
    start_g(1, 0, (L1, R2))

    exchange(1)
    first_chunk(1)

    lane128 = lax.broadcasted_iota(jnp.int32, (TILE, HALF), 1)

    def last_tile(t, carry):
        logits = temp_c[t] * mixed(t, acc[t] + product(1, 1, t))
        top = jnp.max(jnp.where(inside, logits, -jnp.inf), axis=1, keepdims=True)
        shifted = jnp.where(inside, logits - top, 0.0)
        expo = jnp.where(inside, jnp.exp(shifted), 0.0)
        acc[t] = expo
        total = jnp.sum(expo, axis=1, keepdims=True)
        moment = jnp.sum(expo * shifted, axis=1, keepdims=True)
        packed = jnp.where(lane128 == 0, top, jnp.where(lane128 == 1, total, moment))
        stats[y, t] = jnp.transpose(packed, (1, 0))[:8, :]
        return carry

    lax.fori_loop(0, TPD, last_tile, 0)

    y_copies = []
    for dy in range(1, 4):
        y_copies.append(
            pltpu.make_async_remote_copy(
                src_ref=stats.at[y], dst_ref=stats.at[y],
                send_sem=y_send.at[dy - 1], recv_sem=y_recv.at[dy - 1],
                device_id=(lax.rem(y + dy, 4), r), device_id_type=MESH,
            )
        )
    for cp in y_copies:
        cp.start()
    for kh in range(2):
        wait_sends(kh, 1)
    for dy in range(1, 4):
        pltpu.make_async_remote_copy(
            src_ref=stats.at[y], dst_ref=stats.at[lax.rem(y + 4 - dy, 4)],
            send_sem=y_send.at[dy - 1], recv_sem=y_recv.at[dy - 1],
            device_id=(lax.rem(y + dy, 4), r), device_id_type=MESH,
        ).wait_recv()
    for cp in y_copies:
        cp.wait_send()

    out_cps = []
    for t in range(TPD):
        parts = [stats[k, t] for k in range(4)]
        tops = [p[0:1, :] for p in parts]
        top = functools.reduce(jnp.maximum, tops)
        total = jnp.zeros((1, TILE), jnp.float32)
        moment = jnp.zeros((1, TILE), jnp.float32)
        for p in parts:
            diff = p[0:1, :] - top
            scale = jnp.exp(diff)
            total = total + scale * p[1:2, :]
            moment = moment + scale * (p[2:3, :] + p[1:2, :] * diff)
        cert = 1.0 - (jnp.log(total) - moment / total) / jnp.log(jnp.float32(CLS))
        cert_ref[2 * t : 2 * t + 1, :] = cert[:, :HALF]
        cert_ref[2 * t + 1 : 2 * t + 2, :] = cert[:, HALF:]
        factor = jnp.exp(stats[y, t][0:1, :] - top) / total
        col = jnp.transpose(jnp.broadcast_to(factor, (8, TILE)), (1, 0))[:, 0:1]
        outv[t * TILE : (t + 1) * TILE, :] = (acc[t] * col).astype(jnp.bfloat16)[:, :W]
        cp = pltpu.make_async_copy(
            outv.at[pl.ds(t * TILE, TILE)], pseudo_hbm.at[pl.ds(t * TILE, TILE)], loc.at[2 + t]
        )
        cp.start()
        out_cps.append(cp)
    for cp in out_cps:
        cp.wait()


def local(prior, blocks, links, counts, fetch, seeds, inv_temp):
    r = lax.axis_index("rows")
    c, x, z = r % 2, (r // 2) % 4, r // 8
    s = jnp.maximum(links - TPD, 0)
    dz = (s // 8 - z) & 3
    dx = ((s // 2) % 4 - x) & 3
    dc = (s - c) & 1
    live = jnp.arange(NB, dtype=jnp.int32)[None, :] < counts[:, None]
    own = links < TPD

    def table(first, second):
        slot = jnp.where(own, 4 * TPD + links, (first * 2 + dc) * 4 + second)
        return jnp.where(live, slot, ZERO).reshape(-1)

    tab_a = table(dz, dx)
    tab_b = table(dx, dz)
    fetch_row = jnp.broadcast_to(jnp.pad(fetch.reshape(1, -1), ((0, 0), (0, 96))), (8, 128))
    bf, f32 = jnp.bfloat16, jnp.float32
    vmem = pltpu.VMEM
    pseudo, cert = pl.pallas_call(
        kernel,
        out_shape=(
            jax.ShapeDtypeStruct((TPD * TILE, W), bf),
            jax.ShapeDtypeStruct((16, 128), f32),
        ),
        in_specs=[
            pl.BlockSpec(memory_space=pltpu.SMEM),
            pl.BlockSpec(memory_space=pltpu.SMEM),
            pl.BlockSpec(memory_space=pltpu.VMEM),
            pl.BlockSpec(memory_space=pl.ANY),
            pl.BlockSpec(memory_space=pl.ANY),
            pl.BlockSpec(memory_space=pltpu.VMEM),
            pl.BlockSpec(memory_space=pltpu.VMEM),
        ],
        out_specs=(pl.BlockSpec(memory_space=pl.ANY), pl.BlockSpec(memory_space=pltpu.VMEM)),
        scratch_shapes=[
            vmem((TPD * TILE, W), bf),
            vmem((TPD, NB, TILE, TILE), bf),
            vmem((TPD, TILE, TILE), f32),
            vmem((TPD, TILE, TILE), bf),
            vmem((TPD, TILE, TILE), bf),
            vmem((4, 7, 4, Q, TILE), bf),
            vmem((16, 8, 128), jnp.int32),
            pltpu.SMEM((16, 8, 128), jnp.int32),
            vmem((TPD, TILE, 1), jnp.int32),
            vmem((TPD, TILE, 1), f32),
            vmem((4, TPD, 8, TILE), f32),
            vmem((TPD * TILE, W), bf),
        ]
        + [vmem((3, TPD, Q, TILE), bf) for _ in range(8)]
        + [vmem((2, 4, Q, TILE), bf) for _ in range(8)]
        + [vmem((ZERO + 1, Q, TILE), bf) for _ in range(8)]
        + [
            pltpu.SemaphoreType.DMA((4, 15)),
            pltpu.SemaphoreType.DMA((8, 15)),
            pltpu.SemaphoreType.DMA((14,)),
            pltpu.SemaphoreType.DMA((14,)),
            pltpu.SemaphoreType.DMA((3,)),
            pltpu.SemaphoreType.DMA((3,)),
            pltpu.SemaphoreType.DMA((TPD,)),
            pltpu.SemaphoreType.DMA((10,)),
        ],
        compiler_params=pltpu.CompilerParams(
            collective_id=0, has_side_effects=True, vmem_limit_bytes=66_000_000
        ),
        name="propagate",
    )(
        tab_a, tab_b, fetch_row, prior, blocks,
        seeds.reshape(16, 128), inv_temp.reshape(16, 128),
    )
    return pseudo, cert.reshape(-1)


def solution(mesh):
    return jax.shard_map(
        local,
        mesh=mesh,
        in_specs=(
            P("rows", "cls"),
            P("rows", None, None, None),
            P("rows", None),
            P("rows"),
            P("rows", None, None),
            P("rows"),
            P("rows"),
        ),
        out_specs=(P("rows", "cls"), P("rows")),
        check_vma=False,
    )
```

time: 285 us -> 121 us (0.42)
  Pallas kernels: 0 us -> 113 us
  waiting for transfers between devices: 108 us -> 0 us
  local copies, waits for them, and re-layouts: 69.3 us -> 6.11 us
  blocking collectives: 40.6 us -> 0 us
  matrix products: 38.2 us -> 0 us
  other arithmetic: 17.1 us -> 0.76 us
  starting transfers between devices: 9.97 us -> 0 us
    pallas_call x0 -> x1, Pallas kernels: none -> 113 us  [local(): pl.pallas_call(kernel, out_shape=(jax.ShapeDtypeStruct((TPD * TILE, W), b...]
    all_to_all x2 -> x0, waiting for transfers between devices: 108 us -> none  [local(): lax.all_to_all(outgoing, 'rows', split_axis=0, concat_axis=0, tiled=True)]
    gather x5 -> x0, local copies, waits for them, and re-layouts: 66.5 us -> none  [the longest x3 59.7 us: propagate_local(): adjacent_blocks = column_set[slot_tiles]]
    dot_general x2 -> x0, matrix products: 38.2 us -> none  [propagate_local(): jnp.einsum('mvfg,mvgx->mfx', blocks, adjacent_blocks, preferred_element_t...]
    all_to_all x1 -> x0, blocking collectives: 15.4 us -> none  [local(): lax.all_to_all(fetch, 'rows', split_axis=1, concat_axis=0, tiled=True)]
    psum x1 -> x0, blocking collectives: 14.3 us -> none  [local(): lax.psum((jnp.sum(expo, axis=1), jnp.sum(expo * shifted, axis=1)), 'cls')]
    pmax x1 -> x0, blocking collectives: 10.8 us -> none  [local(): top = lax.pmax(jnp.max(logits, axis=1), 'cls')]
    concatenate x2 -> x0, other arithmetic: 10.5 us -> none  [local(): jnp.concatenate([tiled, arrived.reshape(-1, tile_rows, col_width)], axis=0)]
  transfers between devices with their start and end apart: 2 -> 0, of which waited for: 2 -> 0; matrix products, arithmetic and copies ran while one was open for 0% -> 0% of each run, Pallas kernels for 0% -> 0%
where the time goes in v1:
time: 121 us
  Pallas kernels  113 us (93%)
  local copies, waits for them, and re-layouts  6.11 us (5%)
    pallas_call x1, Pallas kernels, local(): pl.pallas_call(kernel, out_shape=(jax.ShapeDtypeStruct((TPD * TILE, W), b...  113 us
    unnamed x2, local copies, waits for them, and re-layouts  3.56 us

profile of v1, /device:TPU:0, one launch (start us, length us, event | category | flops | bytes accessed | tf_op | source)
XLA Modules:
  0.0 120.6 jit_solution(901564232761604214)
XLA Ops:
  0.7 0.7 pad_bitcast_fusion
  1.3 0.6 broadcast_in_dim.16.fetch_row
  1.9 0.8 select_select_fusion
  2.7 0.7 reshape.24.tab_b
  3.3 0.6 reshape.23.tab_a
  4.0 113.0 %propagate.1 = (bf16[2048,250]{1,0:T(8,128)(2,1)}, f32[16,128]{1,0:T(8,128)}) custom-call(s32[192]{0:T(256)} %reshape.23.tab_a, s32[192]{0:T(256)} %reshape.24.tab_b, s32[8,128]{1,0:T(8,128)} %broadcast_in_dim.16.fetch_row, bf16[2048,250]{1,0:T(8,128)(2,1)} %prior_hbm.1, bf16[8,24,256,256]{3,2,1,0:T(8,128)(2,1)} %blocks_hbm.1, s32[16,128]{1,0:T(8,128)} %bitcast.6, ...), custom_call_target="tpu_custom_call" | custom-call | tf_op jit(solution)/shard_map/propagate/pallas_call | solution.py:386
  117.0 2.3 %copy.11 = bf16[2048,250]{1,0:T(8,128)(2,1)} copy(bf16[2048,250]{1,0:T(8,128)(2,1)} %get-tuple-element.10) | data formatting | bytes 2048000
  119.3 1.3 %copy.12 = f32[2048]{0:T(1024)} copy(f32[2048]{0:T(1024)} %bitcast.8) | data formatting | bytes 16384

commit v2 on v1

--- a/solution.py
+++ b/solution.py
@@ -20,7 +20,9 @@
 BLEND = 0.8
 MESH = pl.DeviceIdType.MESH
 
-R1, R2, L1, L2, FR, FL, RR, RL, D0R, D1R, D0L, D1L, WR, WL, PT = range(15)
+GR, GL, FR, FL = (0, 1, 2, 3), (4, 5, 6, 7), (8, 9), (10, 11)
+RR, RL, D0R, D1R, D0L, D1L, WR, WL, PT = range(12, 21)
+NAMES = 21
 
 PEERS = [(0, dz, dc) for dz in range(4) for dc in range(2) if (dz, dc) != (0, 0)] + [
     (dx, 0, dc) for dx in range(1, 4) for dc in range(2)
@@ -28,15 +30,16 @@
 
 
 def kernel(
-    tab_a, tab_b, fetch_row, prior_hbm, blocks_hbm, seeds_ref, temp_ref,
-    pseudo_hbm, cert_ref,
+    links_ref, counts_ref, fetch_ref, prior_hbm, blocks_hbm, seeds_ref, temp_ref,
+    expo_hbm, stats_out,
     *scratch,
 ):
-    (pv, bv, acc, fld0, fld1, stage, frv, frm, seed_c, temp_c, stats, outv) = scratch[:12]
-    gb = scratch[12:20]
-    rl = scratch[20:28]
-    cs = scratch[28:36]
-    (send, recv, f_send, f_recv, y_send, y_recv, b_sem, loc) = scratch[36:]
+    (pv, bv, acc, raw, fld0, fld1, stage, frv, frm, tab_a, tab_b, seed_c, temp_c) = scratch[:13]
+    expos, stats = scratch[13:15]
+    gb = scratch[15:23]
+    rl = scratch[23:31]
+    cs = scratch[31:39]
+    (send, recv, f_send, f_recv, y_send, y_recv, b_sem, loc) = scratch[39:]
     fld = (fld0, fld1)
 
     r = lax.axis_index("rows")
@@ -70,8 +73,10 @@
         pl.semaphore_signal(
             barrier, inc=1, device_id=(lax.rem(y + dy, 4), r), device_id_type=MESH
         )
-    frv[0] = fetch_row[...]
-    frv[8] = fetch_row[...]
+    frv[0] = jnp.zeros((8, 128), jnp.int32)
+    frv[0, 0:1, 0:32] = fetch_ref[...]
+    frv[8] = jnp.zeros((8, 128), jnp.int32)
+    frv[8, 0:1, 0:32] = fetch_ref[...]
     prior_cp.wait()
     for t in range(TPD):
         fld0[t, :, HALF:] = jnp.zeros((TILE, HALF), jnp.bfloat16)
@@ -80,17 +85,15 @@
 
     def g_copy(rnd, rt, kh, name):
         i = idx(rnd, rt, kh)
-        lo, hi = slice(0, 4), slice(4, 8)
         rows = pl.ds(kh * HALF + rt * Q, Q)
-        own = fld[rnd]
-        src, dst, d = {
-            R1: (own.at[lo, rows, :], gb[i].at[2, lo], 1),
-            R2: (own.at[hi, rows, :], gb[i].at[2, hi], 1),
-            L1: (own.at[hi, rows, :], gb[i].at[0, hi], -1),
-            L2: (own.at[lo, rows, :], gb[i].at[0, lo], -1),
-            FR: (gb[i].at[2, lo], gb[i].at[1, lo], 1),
-            FL: (gb[i].at[0, hi], gb[i].at[1, hi], -1),
-        }[name]
+        if name in GR or name in GL:
+            pair = pl.ds(2 * (name % 4), 2)
+            d, far = (1, 2) if name in GR else (-1, 0)
+            src, dst = fld[rnd].at[pair, rows, :], gb[i].at[far, pair]
+        else:
+            d, far = (1, 2) if name in FR else (-1, 0)
+            pair = pl.ds(2 * (name - 8), 2)
+            src, dst = gb[i].at[far, pair], gb[i].at[1, pair]
         return pltpu.make_async_remote_copy(
             src_ref=src, dst_ref=dst, send_sem=send.at[idx(0, rt, kh), name],
             recv_sem=recv.at[i, name], device_id=gstep(rt, d), device_id_type=MESH,
@@ -139,7 +142,7 @@
 
     def wait_sends(kh, rnd):
         for rt in range(2):
-            for name in (R1, R2, L1, L2, FR, FL):
+            for name in GR + GL + FR + FL:
                 g_copy(rnd, rt, kh, name).wait_send()
             for name in (RR, RL, D0R, D1R, D0L, D1L, WR, WL, PT):
                 p_copy(rnd, rt, kh, name).wait_send()
@@ -152,7 +155,7 @@
         d = dz if base == 0 else dx
         f_copies.append(
             pltpu.make_async_remote_copy(
-                src_ref=fetch_row, dst_ref=frv.at[base + ((4 - d) % 4) * 2 + dc],
+                src_ref=frv.at[0], dst_ref=frv.at[base + ((4 - d) % 4) * 2 + dc],
                 send_sem=f_send.at[k], recv_sem=f_recv.at[k],
                 device_id=dev(dx, dz, dc), device_id_type=MESH,
             )
@@ -210,17 +213,17 @@
         hit = (seed_c[t] == column) & inside
         return BLEND * total + jnp.where(hit, jnp.float32(1.0 - BLEND), jnp.float32(0.0))
 
-    HOP1 = (R1, L1)
-    HOP1B = (R2, L2)
-    FWD = (FR, FL)
+    HOP = ((GR[0], GL[0]), (GR[2], GL[2]), (GR[1], GL[1]), (GR[3], GL[3]))
+    ALL_HOPS = sum(HOP, ())
+    GO_ON = (((GR[0], FR[0]), (GL[2], FL[0])), ((GR[1], FR[1]), (GL[3], FL[1])))
+    REST = (GR[2], GR[3], GL[0], GL[1]) + FR + FL
     SENDS = (RR, RL, D0R, D0L, D1R, D1L, PT)
     RELAY = (WR, WL)
     FINAL = (D0R, D0L, D1R, D1L, PT, WR, WL)
 
-    start_g(0, 0, HOP1)
     for cp in f_copies:
         cp.start()
-    start_g(0, 0, HOP1B)
+    start_g(0, 0, ALL_HOPS)
     for cp in block_cps:
         cp.start()
 
@@ -230,32 +233,58 @@
                 cs[idx(rnd, rt, kh)][ZERO] = jnp.zeros((Q, TILE), jnp.bfloat16)
     for t in range(TPD):
         own_slots(0, t)
-    seeds_t = jnp.transpose(seeds_ref[...].astype(jnp.float32), (1, 0))
-    temps_t = jnp.transpose(temp_ref[...], (1, 0))
-    for t in range(TPD):
-        for h in range(2):
-            k = 2 * t + h
-            seed_c[t, h * HALF : (h + 1) * HALF, :] = seeds_t[:, k : k + 1].astype(jnp.int32)
-            temp_c[t, h * HALF : (h + 1) * HALF, :] = temps_t[:, k : k + 1]
-    for cp in f_copies:
-        cp.wait()
-    to_smem = pltpu.make_async_copy(frv, frm, loc.at[1])
-    to_smem.start()
-    to_smem.wait()
+
+    def forward(rnd, kh):
+        for part in GO_ON:
+            for name, onward in part:
+                wait_g(rnd, kh, (name,))
+                start_g(rnd, kh, (onward,))
+
+    def prepare():
+        seeds_t = jnp.transpose(seeds_ref[...].astype(jnp.float32), (1, 0))
+        temps_t = jnp.transpose(temp_ref[...], (1, 0))
+        for t in range(TPD):
+            for h in range(2):
+                k = 2 * t + h
+                seed_c[t, h * HALF : (h + 1) * HALF, :] = seeds_t[:, k : k + 1].astype(jnp.int32)
+                temp_c[t, h * HALF : (h + 1) * HALF, :] = temps_t[:, k : k + 1]
+        for cp in f_copies:
+            cp.wait()
+        to_smem = pltpu.make_async_copy(frv, frm, loc.at[1])
+        to_smem.start()
+
+        def slots(t, carry):
+            count = counts_ref[t]
+            for j in range(NB):
+                v = links_ref[t, j]
+                s = jnp.maximum(v - TPD, 0)
+                dz = ((s >> 3) + 4 - z) & 3
+                dx = (((s >> 1) & 3) + 4 - x) & 3
+                dc = (s + c) & 1
+                own = v < TPD
+                live = j < count
+                sa = jnp.where(own, 4 * TPD + v, (dz * 2 + dc) * 4 + dx)
+                sb = jnp.where(own, 4 * TPD + v, (dx * 2 + dc) * 4 + dz)
+                tab_a[t * NB + j] = jnp.where(live, sa, ZERO)
+                tab_b[t * NB + j] = jnp.where(live, sb, ZERO)
+            return carry
+
+        lax.fori_loop(0, TPD, slots, 0)
+        to_smem.wait()
 
     def exchange(rnd):
-        wait_g(rnd, 0, HOP1)
-        start_g(rnd, 0, FWD)
-        start_g(rnd, 1, HOP1 + HOP1B)
-        wait_g(rnd, 0, HOP1B + FWD)
+        forward(rnd, 0)
+        start_g(rnd, 1, ALL_HOPS)
+        if rnd == 0:
+            prepare()
+        wait_g(rnd, 0, REST)
         select(rnd, 0)
+        forward(rnd, 1)
         start_p(rnd, 0, SENDS)
-        wait_g(rnd, 1, HOP1)
-        start_g(rnd, 1, FWD)
+        wait_g(rnd, 1, REST)
+        select(rnd, 1)
         wait_p(rnd, 0, (RR, RL))
         start_p(rnd, 0, RELAY)
-        wait_g(rnd, 1, HOP1B + FWD)
-        select(rnd, 1)
         start_p(rnd, 1, SENDS)
         wait_p(rnd, 0, FINAL)
 
@@ -279,69 +308,100 @@
     for kh in range(2):
         wait_sends(kh, 0)
 
-    def first_tile(t, carry):
+    def first_tile(i, carry):
+        for k in range(3):
+
+            @pl.when(i == 2 * k + 2)
+            def _():
+                start_g(1, 0, HOP[k])
+
+        t = (i // 4) * 2 + ((i // 2) % 2) * 4 + i % 2
         value = mixed(t, acc[t] + product(0, 1, t)).astype(jnp.bfloat16)
         fld1[t] = value
         for rt in range(2):
             for kh in range(2):
                 a = kh * HALF + rt * Q
                 cs[idx(1, rt, kh)][4 * TPD + t] = value[a : a + Q, :]
-
-        @pl.when(t == 3)
-        def _():
-            start_g(1, 0, (R1, L2))
-
         return carry
 
     lax.fori_loop(0, TPD, first_tile, 0)
-    start_g(1, 0, (L1, R2))
+    start_g(1, 0, HOP[3])
 
     exchange(1)
     first_chunk(1)
 
     lane128 = lax.broadcasted_iota(jnp.int32, (TILE, HALF), 1)
 
-    def last_tile(t, carry):
-        logits = temp_c[t] * mixed(t, acc[t] + product(1, 1, t))
+    def softmax(t):
+        logits = temp_c[t] * mixed(t, raw[...])
         top = jnp.max(jnp.where(inside, logits, -jnp.inf), axis=1, keepdims=True)
         shifted = jnp.where(inside, logits - top, 0.0)
         expo = jnp.where(inside, jnp.exp(shifted), 0.0)
-        acc[t] = expo
         total = jnp.sum(expo, axis=1, keepdims=True)
         moment = jnp.sum(expo * shifted, axis=1, keepdims=True)
         packed = jnp.where(lane128 == 0, top, jnp.where(lane128 == 1, total, moment))
-        stats[y, t] = jnp.transpose(packed, (1, 0))[:8, :]
+        return expo, jnp.transpose(packed, (1, 0))[:8, :]
+
+    def keep(t, expo, stat):
+        expos[t] = expo
+        stats[y, t] = stat
+
+    def y_copy(dy, half, slot):
+        tiles = pl.ds(4 * half, 4)
+        k = 2 * (dy - 1) + half
+        return pltpu.make_async_remote_copy(
+            src_ref=stats.at[y, tiles], dst_ref=stats.at[slot, tiles],
+            send_sem=y_send.at[k], recv_sem=y_recv.at[k],
+            device_id=(lax.rem(y + dy, 4), r), device_id_type=MESH,
+        )
+
+    def out_copy(t):
+        return pltpu.make_async_copy(expos.at[t], expo_hbm.at[t], loc.at[2 + t])
+
+    def last_tile(t, carry):
+        before = jnp.maximum(t - 1, 0)
+        expo, stat = softmax(before)
+        total = acc[t] + product(1, 1, t)
+        keep(before, expo, stat)
+        raw[...] = total
+
+        @pl.when(t == 5)
+        def _():
+            for dy in (2, 1, 3):
+                y_copy(dy, 0, y).start()
+            for k in range(4):
+                out_copy(k).start()
+
         return carry
 
+    raw[...] = jnp.zeros((TILE, TILE), jnp.float32)
     lax.fori_loop(0, TPD, last_tile, 0)
-
-    y_copies = []
-    for dy in range(1, 4):
-        y_copies.append(
-            pltpu.make_async_remote_copy(
-                src_ref=stats.at[y], dst_ref=stats.at[y],
-                send_sem=y_send.at[dy - 1], recv_sem=y_recv.at[dy - 1],
-                device_id=(lax.rem(y + dy, 4), r), device_id_type=MESH,
-            )
-        )
-    for cp in y_copies:
-        cp.start()
+    keep(TPD - 1, *softmax(TPD - 1))
+    for dy in (2, 1, 3):
+        y_copy(dy, 1, y).start()
+    for k in range(4, TPD):
+        out_copy(k).start()
     for kh in range(2):
         wait_sends(kh, 1)
-    for dy in range(1, 4):
-        pltpu.make_async_remote_copy(
-            src_ref=stats.at[y], dst_ref=stats.at[lax.rem(y + 4 - dy, 4)],
-            send_sem=y_send.at[dy - 1], recv_sem=y_recv.at[dy - 1],
-            device_id=(lax.rem(y + dy, 4), r), device_id_type=MESH,
-        ).wait_recv()
-    for cp in y_copies:
-        cp.wait_send()
-
-    out_cps = []
+    for k in range(TPD):
+        out_copy(k).wait()
+    for half in range(2):
+        for dy in range(1, 4):
+            y_copy(dy, half, y).wait_send()
+            y_copy(dy, half, lax.rem(y + 4 - dy, 4)).wait_recv()
+    stats_out[...] = stats[...]
+
+
+def finish(expo_hbm, stats, pseudo_hbm, cert_ref, ev, outv, sem_in, sem_out):
+    y = lax.axis_index("cls")
+    copies_in, copies_out = [], []
+    for t in range(TPD):
+        cp = pltpu.make_async_copy(expo_hbm.at[t], ev.at[t], sem_in.at[t])
+        cp.start()
+        copies_in.append(cp)
     for t in range(TPD):
         parts = [stats[k, t] for k in range(4)]
-        tops = [p[0:1, :] for p in parts]
-        top = functools.reduce(jnp.maximum, tops)
+        top = functools.reduce(jnp.maximum, [p[0:1, :] for p in parts])
         total = jnp.zeros((1, TILE), jnp.float32)
         moment = jnp.zeros((1, TILE), jnp.float32)
         for p in parts:
@@ -354,40 +414,26 @@
         cert_ref[2 * t + 1 : 2 * t + 2, :] = cert[:, HALF:]
         factor = jnp.exp(stats[y, t][0:1, :] - top) / total
         col = jnp.transpose(jnp.broadcast_to(factor, (8, TILE)), (1, 0))[:, 0:1]
-        outv[t * TILE : (t + 1) * TILE, :] = (acc[t] * col).astype(jnp.bfloat16)[:, :W]
+        copies_in[t].wait()
+        rows = slice(t * TILE, (t + 1) * TILE)
+        outv[rows, :] = (ev[t] * col).astype(jnp.bfloat16)[:, :W]
         cp = pltpu.make_async_copy(
-            outv.at[pl.ds(t * TILE, TILE)], pseudo_hbm.at[pl.ds(t * TILE, TILE)], loc.at[2 + t]
+            outv.at[pl.ds(t * TILE, TILE)], pseudo_hbm.at[pl.ds(t * TILE, TILE)], sem_out.at[t]
         )
         cp.start()
-        out_cps.append(cp)
-    for cp in out_cps:
+        copies_out.append(cp)
+    for cp in copies_out:
         cp.wait()
 
 
 def local(prior, blocks, links, counts, fetch, seeds, inv_temp):
-    r = lax.axis_index("rows")
-    c, x, z = r % 2, (r // 2) % 4, r // 8
-    s = jnp.maximum(links - TPD, 0)
-    dz = (s // 8 - z) & 3
-    dx = ((s // 2) % 4 - x) & 3
-    dc = (s - c) & 1
-    live = jnp.arange(NB, dtype=jnp.int32)[None, :] < counts[:, None]
-    own = links < TPD
-
-    def table(first, second):
-        slot = jnp.where(own, 4 * TPD + links, (first * 2 + dc) * 4 + second)
-        return jnp.where(live, slot, ZERO).reshape(-1)
-
-    tab_a = table(dz, dx)
-    tab_b = table(dx, dz)
-    fetch_row = jnp.broadcast_to(jnp.pad(fetch.reshape(1, -1), ((0, 0), (0, 96))), (8, 128))
     bf, f32 = jnp.bfloat16, jnp.float32
     vmem = pltpu.VMEM
-    pseudo, cert = pl.pallas_call(
+    expo, stats = pl.pallas_call(
         kernel,
         out_shape=(
-            jax.ShapeDtypeStruct((TPD * TILE, W), bf),
-            jax.ShapeDtypeStruct((16, 128), f32),
+            jax.ShapeDtypeStruct((TPD, TILE, TILE), f32),
+            jax.ShapeDtypeStruct((4, TPD, 8, TILE), f32),
         ),
         in_specs=[
             pl.BlockSpec(memory_space=pltpu.SMEM),
@@ -403,26 +449,29 @@
             vmem((TPD * TILE, W), bf),
             vmem((TPD, NB, TILE, TILE), bf),
             vmem((TPD, TILE, TILE), f32),
+            vmem((TILE, TILE), f32),
             vmem((TPD, TILE, TILE), bf),
             vmem((TPD, TILE, TILE), bf),
             vmem((4, 7, 4, Q, TILE), bf),
             vmem((16, 8, 128), jnp.int32),
             pltpu.SMEM((16, 8, 128), jnp.int32),
+            pltpu.SMEM((TPD * NB,), jnp.int32),
+            pltpu.SMEM((TPD * NB,), jnp.int32),
             vmem((TPD, TILE, 1), jnp.int32),
             vmem((TPD, TILE, 1), f32),
+            vmem((TPD, TILE, TILE), f32),
             vmem((4, TPD, 8, TILE), f32),
-            vmem((TPD * TILE, W), bf),
         ]
         + [vmem((3, TPD, Q, TILE), bf) for _ in range(8)]
         + [vmem((2, 4, Q, TILE), bf) for _ in range(8)]
         + [vmem((ZERO + 1, Q, TILE), bf) for _ in range(8)]
         + [
-            pltpu.SemaphoreType.DMA((4, 15)),
-            pltpu.SemaphoreType.DMA((8, 15)),
+            pltpu.SemaphoreType.DMA((4, NAMES)),
+            pltpu.SemaphoreType.DMA((8, NAMES)),
             pltpu.SemaphoreType.DMA((14,)),
             pltpu.SemaphoreType.DMA((14,)),
-            pltpu.SemaphoreType.DMA((3,)),
-            pltpu.SemaphoreType.DMA((3,)),
+            pltpu.SemaphoreType.DMA((6,)),
+            pltpu.SemaphoreType.DMA((6,)),
             pltpu.SemaphoreType.DMA((TPD,)),
             pltpu.SemaphoreType.DMA((10,)),
         ],
@@ -431,9 +480,28 @@
         ),
         name="propagate",
     )(
-        tab_a, tab_b, fetch_row, prior, blocks,
+        links, counts, fetch.reshape(1, -1), prior, blocks,
         seeds.reshape(16, 128), inv_temp.reshape(16, 128),
     )
+    pseudo, cert = pl.pallas_call(
+        finish,
+        out_shape=(
+            jax.ShapeDtypeStruct((TPD * TILE, W), bf),
+            jax.ShapeDtypeStruct((16, 128), f32),
+        ),
+        in_specs=[
+            pl.BlockSpec(memory_space=pl.ANY),
+            pl.BlockSpec(memory_space=pltpu.VMEM),
+        ],
+        out_specs=(pl.BlockSpec(memory_space=pl.ANY), pl.BlockSpec(memory_space=pltpu.VMEM)),
+        scratch_shapes=[
+            vmem((TPD, TILE, TILE), f32),
+            vmem((TPD * TILE, W), bf),
+            pltpu.SemaphoreType.DMA((TPD,)),
+            pltpu.SemaphoreType.DMA((TPD,)),
+        ],
+        name="finish",
+    )(expo, stats)
     return pseudo, cert.reshape(-1)
 
 

time: 121 us -> 112 us (0.926)
  local copies, waits for them, and re-layouts: 6.11 us -> 0 us
  Pallas kernels: 113 us -> 111 us
    unnamed x2 -> x0, local copies, waits for them, and re-layouts: 3.56 us -> none
    pallas_call x1 -> x2, Pallas kernels: 113 us -> 111 us  [the longest x1 106 us: local(): pl.pallas_call(kernel, out_shape=(jax.ShapeDtypeStruct((TPD, TILE, TILE),...]
    reshape x2 -> x0, local copies, waits for them, and re-layouts: 1.3 us -> none  [table(): return jnp.where(live, slot, ZERO).reshape(-1)]
    broadcast_in_dim x2 -> x0, local copies, waits for them, and re-layouts: 1.26 us -> none  [local(): jnp.broadcast_to(jnp.pad(fetch.reshape(1, -1), ((0, 0), (0, 96))), (8, 128))]
where the time goes in v2:
time: 112 us; the launch traced here: 111 us
  Pallas kernels  111 us (99%)
    pallas_call x1, Pallas kernels, local(): pl.pallas_call(kernel, out_shape=(jax.ShapeDtypeStruct((TPD, TILE, TILE),...  106 us
    pallas_call x1, Pallas kernels, local(): pl.pallas_call(finish, out_shape=(jax.ShapeDtypeStruct((TPD * TILE, W), b...  4.6 us

profile of v2, /device:TPU:0, one launch (start us, length us, event | category | flops | bytes accessed | tf_op | source)
XLA Modules:
  0.0 111.3 jit_solution(17922918692940812646)
XLA Ops:
  0.6 106.0 %propagate.1 = (f32[8,256,256]{2,1,0:T(8,128)}, f32[4,8,8,256]{3,2,1,0:T(8,128)}) custom-call(s32[8,24]{1,0:T(8,128)} %links_ref.1, s32[8]{0:T(128)} %counts_ref.1, s32[1,32]{1,0:T(1,128)} %bitcast.6, bf16[2048,250]{1,0:T(8,128)(2,1)} %prior_hbm.1, bf16[8,24,256,256]{3,2,1,0:T(8,128)(2,1)} %blocks_hbm.1, s32[16,128]{1,0:T(8,128)} %bitcast.4, f32[16,128]{1,0:T(8,128)} %bitcast.5), custom_call_target="tpu_custom_call" | custom-call | tf_op jit(solution)/shard_map/propagate/pallas_call | solution.py:432
  106.7 4.6 %finish.1 = (bf16[2048,250]{1,0:T(8,128)(2,1)}, f32[16,128]{1,0:T(8,128)}) custom-call(f32[8,256,256]{2,1,0:T(8,128)} %get-tuple-element.6.expo_hbm, f32[4,8,8,256]{3,2,1,0:T(8,128)} %get-tuple-element.7.stats), custom_call_target="tpu_custom_call" | custom-call | tf_op jit(solution)/shard_map/finish/pallas_call | solution.py:486

commit v3 on v2

--- a/solution.py
+++ b/solution.py
@@ -15,6 +15,7 @@
 W = 250
 HALF = 128
 Q = 64
+VLIM = 66_000_000
 ZERO = 40
 
 BLEND = 0.8
@@ -30,16 +31,17 @@
 
 
 def kernel(
-    links_ref, counts_ref, fetch_ref, prior_hbm, blocks_hbm, seeds_ref, temp_ref,
+    links_hbm, counts_hbm, fetch_hbm, prior_hbm, blocks_hbm, seeds_hbm, temp_hbm,
     expo_hbm, stats_out,
     *scratch,
 ):
-    (pv, bv, acc, raw, fld0, fld1, stage, frv, frm, tab_a, tab_b, seed_c, temp_c) = scratch[:13]
-    expos, stats = scratch[13:15]
-    gb = scratch[15:23]
-    rl = scratch[23:31]
-    cs = scratch[31:39]
-    (send, recv, f_send, f_recv, y_send, y_recv, b_sem, loc) = scratch[39:]
+    (pv, bv, acc, raw, fld0, fld1, stage, frv, frm, tab_a, tab_b, seed_c, temp_r) = scratch[:13]
+    expos, stats, seed_r = scratch[13:16]
+    links_ref, counts_ref, fetch_ref, seeds_ref, temp_ref, small = scratch[-6:]
+    gb = scratch[16:24]
+    rl = scratch[24:32]
+    cs = scratch[32:40]
+    (send, recv, f_send, f_recv, y_send, y_recv, b_sem, loc) = scratch[40:-6]
     fld = (fld0, fld1)
 
     r = lax.axis_index("rows")
@@ -61,8 +63,6 @@
     def gstep(rt, d):
         return dev(d % 4, 0, 0) if rt == 0 else dev(0, d % 4, 0)
 
-    prior_cp = pltpu.make_async_copy(prior_hbm, pv, loc.at[0])
-    prior_cp.start()
     block_cps = [
         pltpu.make_async_copy(blocks_hbm.at[t], bv.at[t], b_sem.at[t]) for t in range(TPD)
     ]
@@ -73,6 +73,20 @@
         pl.semaphore_signal(
             barrier, inc=1, device_id=(lax.rem(y + dy, 4), r), device_id_type=MESH
         )
+    prior_cp = pltpu.make_async_copy(prior_hbm, pv, loc.at[0])
+    prior_cp.start()
+    small_cps = [
+        pltpu.make_async_copy(src, dst, small.at[k])
+        for k, (src, dst) in enumerate(
+            [
+                (fetch_hbm, fetch_ref), (links_hbm, links_ref), (counts_hbm, counts_ref),
+                (seeds_hbm, seeds_ref), (temp_hbm, temp_ref),
+            ]
+        )
+    ]
+    for cp in small_cps:
+        cp.start()
+    small_cps[0].wait()
     frv[0] = jnp.zeros((8, 128), jnp.int32)
     frv[0, 0:1, 0:32] = fetch_ref[...]
     frv[8] = jnp.zeros((8, 128), jnp.int32)
@@ -241,13 +255,16 @@
                 start_g(rnd, kh, (onward,))
 
     def prepare():
+        for cp in small_cps[1:]:
+            cp.wait()
         seeds_t = jnp.transpose(seeds_ref[...].astype(jnp.float32), (1, 0))
-        temps_t = jnp.transpose(temp_ref[...], (1, 0))
         for t in range(TPD):
             for h in range(2):
                 k = 2 * t + h
                 seed_c[t, h * HALF : (h + 1) * HALF, :] = seeds_t[:, k : k + 1].astype(jnp.int32)
-                temp_c[t, h * HALF : (h + 1) * HALF, :] = temps_t[:, k : k + 1]
+                half = slice(h * HALF, (h + 1) * HALF)
+                seed_r[t : t + 1, half] = seeds_ref[k : k + 1, :]
+                temp_r[t : t + 1, half] = temp_ref[k : k + 1, :]
         for cp in f_copies:
             cp.wait()
         to_smem = pltpu.make_async_copy(frv, frm, loc.at[1])
@@ -330,28 +347,33 @@
     exchange(1)
     first_chunk(1)
 
-    lane128 = lax.broadcasted_iota(jnp.int32, (TILE, HALF), 1)
+    class_no = lax.broadcasted_iota(jnp.int32, (TILE, TILE), 0)
+    real = class_no < W
+    class_no = class_no + y * W
 
     def softmax(t):
-        logits = temp_c[t] * mixed(t, raw[...])
-        top = jnp.max(jnp.where(inside, logits, -jnp.inf), axis=1, keepdims=True)
-        shifted = jnp.where(inside, logits - top, 0.0)
-        expo = jnp.where(inside, jnp.exp(shifted), 0.0)
-        total = jnp.sum(expo, axis=1, keepdims=True)
-        moment = jnp.sum(expo * shifted, axis=1, keepdims=True)
-        packed = jnp.where(lane128 == 0, top, jnp.where(lane128 == 1, total, moment))
-        return expo, jnp.transpose(packed, (1, 0))[:8, :]
+        total = jnp.transpose(raw[...], (1, 0))
+        hit = (seed_r[pl.ds(t, 1), :] == class_no) & real
+        total = BLEND * total + jnp.where(hit, jnp.float32(1.0 - BLEND), jnp.float32(0.0))
+        logits = temp_r[pl.ds(t, 1), :] * total
+        top = jnp.max(jnp.where(real, logits, -jnp.inf), axis=0, keepdims=True)
+        shifted = jnp.where(real, logits - top, 0.0)
+        expo = jnp.where(real, jnp.exp(shifted), 0.0)
+        return expo, (
+            top,
+            jnp.sum(expo, axis=0, keepdims=True),
+            jnp.sum(expo * shifted, axis=0, keepdims=True),
+        )
 
     def keep(t, expo, stat):
-        expos[t] = expo
-        stats[y, t] = stat
-
-    def y_copy(dy, half, slot):
-        tiles = pl.ds(4 * half, 4)
-        k = 2 * (dy - 1) + half
+        expos[t] = jnp.transpose(expo, (1, 0)).astype(jnp.bfloat16)
+        for k in range(3):
+            stats[y, k, pl.ds(t, 1), :] = stat[k]
+
+    def y_copy(dy, slot):
         return pltpu.make_async_remote_copy(
-            src_ref=stats.at[y, tiles], dst_ref=stats.at[slot, tiles],
-            send_sem=y_send.at[k], recv_sem=y_recv.at[k],
+            src_ref=stats.at[y], dst_ref=stats.at[slot],
+            send_sem=y_send.at[dy - 1], recv_sem=y_recv.at[dy - 1],
             device_id=(lax.rem(y + dy, 4), r), device_id_type=MESH,
         )
 
@@ -367,8 +389,6 @@
 
         @pl.when(t == 5)
         def _():
-            for dy in (2, 1, 3):
-                y_copy(dy, 0, y).start()
             for k in range(4):
                 out_copy(k).start()
 
@@ -378,50 +398,54 @@
     lax.fori_loop(0, TPD, last_tile, 0)
     keep(TPD - 1, *softmax(TPD - 1))
     for dy in (2, 1, 3):
-        y_copy(dy, 1, y).start()
+        y_copy(dy, y).start()
     for k in range(4, TPD):
         out_copy(k).start()
     for kh in range(2):
         wait_sends(kh, 1)
     for k in range(TPD):
         out_copy(k).wait()
-    for half in range(2):
-        for dy in range(1, 4):
-            y_copy(dy, half, y).wait_send()
-            y_copy(dy, half, lax.rem(y + 4 - dy, 4)).wait_recv()
-    stats_out[...] = stats[...]
-
-
-def finish(expo_hbm, stats, pseudo_hbm, cert_ref, ev, outv, sem_in, sem_out):
+    for dy in range(1, 4):
+        y_copy(dy, y).wait_send()
+        y_copy(dy, lax.rem(y + 4 - dy, 4)).wait_recv()
+    stats_cp = pltpu.make_async_copy(stats, stats_out, loc.at[1])
+    stats_cp.start()
+    stats_cp.wait()
+
+
+def finish(expo_hbm, stats_hbm, pseudo_hbm, cert_ref, ev, outv, stats, sem_in, sem_out):
     y = lax.axis_index("cls")
+    stats_cp = pltpu.make_async_copy(stats_hbm, stats, sem_in.at[TPD])
+    stats_cp.start()
     copies_in, copies_out = [], []
     for t in range(TPD):
         cp = pltpu.make_async_copy(expo_hbm.at[t], ev.at[t], sem_in.at[t])
         cp.start()
         copies_in.append(cp)
+    stats_cp.wait()
+    top = functools.reduce(jnp.maximum, [stats[k, 0] for k in range(4)])
+    total = jnp.zeros((TPD, TILE), jnp.float32)
+    moment = jnp.zeros((TPD, TILE), jnp.float32)
+    for k in range(4):
+        diff = stats[k, 0] - top
+        scale = jnp.exp(diff)
+        total = total + scale * stats[k, 1]
+        moment = moment + scale * (stats[k, 2] + stats[k, 1] * diff)
+    factor = jnp.transpose(jnp.exp(stats[y, 0] - top) / total, (1, 0))
     for t in range(TPD):
-        parts = [stats[k, t] for k in range(4)]
-        top = functools.reduce(jnp.maximum, [p[0:1, :] for p in parts])
-        total = jnp.zeros((1, TILE), jnp.float32)
-        moment = jnp.zeros((1, TILE), jnp.float32)
-        for p in parts:
-            diff = p[0:1, :] - top
-            scale = jnp.exp(diff)
-            total = total + scale * p[1:2, :]
-            moment = moment + scale * (p[2:3, :] + p[1:2, :] * diff)
-        cert = 1.0 - (jnp.log(total) - moment / total) / jnp.log(jnp.float32(CLS))
-        cert_ref[2 * t : 2 * t + 1, :] = cert[:, :HALF]
-        cert_ref[2 * t + 1 : 2 * t + 2, :] = cert[:, HALF:]
-        factor = jnp.exp(stats[y, t][0:1, :] - top) / total
-        col = jnp.transpose(jnp.broadcast_to(factor, (8, TILE)), (1, 0))[:, 0:1]
         copies_in[t].wait()
         rows = slice(t * TILE, (t + 1) * TILE)
-        outv[rows, :] = (ev[t] * col).astype(jnp.bfloat16)[:, :W]
+        part = ev[t].astype(jnp.float32) * factor[:, t : t + 1]
+        outv[rows, :] = part.astype(jnp.bfloat16)[:, :W]
         cp = pltpu.make_async_copy(
             outv.at[pl.ds(t * TILE, TILE)], pseudo_hbm.at[pl.ds(t * TILE, TILE)], sem_out.at[t]
         )
         cp.start()
         copies_out.append(cp)
+    cert = 1.0 - (jnp.log(total) - moment / total) / jnp.log(jnp.float32(CLS))
+    for t in range(TPD):
+        cert_ref[2 * t : 2 * t + 1, :] = cert[t : t + 1, :HALF]
+        cert_ref[2 * t + 1 : 2 * t + 2, :] = cert[t : t + 1, HALF:]
     for cp in copies_out:
         cp.wait()
 
@@ -432,19 +456,11 @@
     expo, stats = pl.pallas_call(
         kernel,
         out_shape=(
-            jax.ShapeDtypeStruct((TPD, TILE, TILE), f32),
-            jax.ShapeDtypeStruct((4, TPD, 8, TILE), f32),
+            jax.ShapeDtypeStruct((TPD, TILE, TILE), bf),
+            jax.ShapeDtypeStruct((4, 3, TPD, TILE), f32),
         ),
-        in_specs=[
-            pl.BlockSpec(memory_space=pltpu.SMEM),
-            pl.BlockSpec(memory_space=pltpu.SMEM),
-            pl.BlockSpec(memory_space=pltpu.VMEM),
-            pl.BlockSpec(memory_space=pl.ANY),
-            pl.BlockSpec(memory_space=pl.ANY),
-            pl.BlockSpec(memory_space=pltpu.VMEM),
-            pl.BlockSpec(memory_space=pltpu.VMEM),
-        ],
-        out_specs=(pl.BlockSpec(memory_space=pl.ANY), pl.BlockSpec(memory_space=pltpu.VMEM)),
+        in_specs=[pl.BlockSpec(memory_space=pl.ANY)] * 7,
+        out_specs=(pl.BlockSpec(memory_space=pl.ANY), pl.BlockSpec(memory_space=pl.ANY)),
         scratch_shapes=[
             vmem((TPD * TILE, W), bf),
             vmem((TPD, NB, TILE, TILE), bf),
@@ -458,9 +474,10 @@
             pltpu.SMEM((TPD * NB,), jnp.int32),
             pltpu.SMEM((TPD * NB,), jnp.int32),
             vmem((TPD, TILE, 1), jnp.int32),
-            vmem((TPD, TILE, 1), f32),
-            vmem((TPD, TILE, TILE), f32),
-            vmem((4, TPD, 8, TILE), f32),
+            vmem((TPD, TILE), f32),
+            vmem((TPD, TILE, TILE), bf),
+            vmem((4, 3, TPD, TILE), f32),
+            vmem((TPD, TILE), jnp.int32),
         ]
         + [vmem((3, TPD, Q, TILE), bf) for _ in range(8)]
         + [vmem((2, 4, Q, TILE), bf) for _ in range(8)]
@@ -470,13 +487,19 @@
             pltpu.SemaphoreType.DMA((8, NAMES)),
             pltpu.SemaphoreType.DMA((14,)),
             pltpu.SemaphoreType.DMA((14,)),
-            pltpu.SemaphoreType.DMA((6,)),
-            pltpu.SemaphoreType.DMA((6,)),
+            pltpu.SemaphoreType.DMA((3,)),
+            pltpu.SemaphoreType.DMA((3,)),
             pltpu.SemaphoreType.DMA((TPD,)),
             pltpu.SemaphoreType.DMA((10,)),
+            pltpu.SMEM((TPD, NB), jnp.int32),
+            pltpu.SMEM((TPD,), jnp.int32),
+            vmem((1, 32), jnp.int32),
+            vmem((16, 128), jnp.int32),
+            vmem((16, 128), f32),
+            pltpu.SemaphoreType.DMA((5,)),
         ],
         compiler_params=pltpu.CompilerParams(
-            collective_id=0, has_side_effects=True, vmem_limit_bytes=66_000_000
+            collective_id=0, has_side_effects=True, vmem_limit_bytes=VLIM
         ),
         name="propagate",
     )(
@@ -491,13 +514,14 @@
         ),
         in_specs=[
             pl.BlockSpec(memory_space=pl.ANY),
-            pl.BlockSpec(memory_space=pltpu.VMEM),
+            pl.BlockSpec(memory_space=pl.ANY),
         ],
         out_specs=(pl.BlockSpec(memory_space=pl.ANY), pl.BlockSpec(memory_space=pltpu.VMEM)),
         scratch_shapes=[
-            vmem((TPD, TILE, TILE), f32),
+            vmem((TPD, TILE, TILE), bf),
             vmem((TPD * TILE, W), bf),
-            pltpu.SemaphoreType.DMA((TPD,)),
+            vmem((4, 3, TPD, TILE), f32),
+            pltpu.SemaphoreType.DMA((TPD + 1,)),
             pltpu.SemaphoreType.DMA((TPD,)),
         ],
         name="finish",

time: 112 us -> 109 us (0.973)
  Pallas kernels: 111 us -> 108 us
    pallas_call x1, Pallas kernels: 106 us -> 104 us  [local(): pl.pallas_call(kernel, out_shape=(jax.ShapeDtypeStruct((TPD, TILE, TILE),...]
    pallas_call x1, Pallas kernels: 4.6 us -> 3.29 us  [local(): pl.pallas_call(finish, out_shape=(jax.ShapeDtypeStruct((TPD * TILE, W), b...]
where the time goes in v3:
time: 109 us; the launch traced here: 108 us
  Pallas kernels  108 us (99%)
    pallas_call x1, Pallas kernels, local(): pl.pallas_call(kernel, out_shape=(jax.ShapeDtypeStruct((TPD, TILE, TILE),...  104 us
    pallas_call x1, Pallas kernels, local(): pl.pallas_call(finish, out_shape=(jax.ShapeDtypeStruct((TPD * TILE, W), b...  3.29 us

profile of v3, /device:TPU:0, one launch (start us, length us, event | category | flops | bytes accessed | tf_op | source)
XLA Modules:
  0.0 108.4 jit_solution(5211251353700981315)
XLA Ops:
  0.6 104.4 %propagate.1 = (bf16[8,256,256]{2,1,0:T(8,128)(2,1)}, f32[4,3,8,256]{3,2,1,0:T(8,128)}) custom-call(s32[8,24]{1,0:T(8,128)} %links_hbm.1, s32[8]{0:T(128)} %counts_hbm.1, s32[1,32]{1,0:T(1,128)} %bitcast.6, bf16[2048,250]{1,0:T(8,128)(2,1)} %prior_hbm.1, bf16[8,24,256,256]{3,2,1,0:T(8,128)(2,1)} %blocks_hbm.1, s32[16,128]{1,0:T(8,128)} %bitcast.4, ...), custom_call_target="tpu_custom_call" | custom-call | tf_op jit(solution)/shard_map/propagate/pallas_call | solution.py:456
  105.1 3.3 %finish.1 = (bf16[2048,250]{1,0:T(8,128)(2,1)}, f32[16,128]{1,0:T(8,128)}) custom-call(bf16[8,256,256]{2,1,0:T(8,128)(2,1)} %get-tuple-element.6.expo_hbm, f32[4,3,8,256]{3,2,1,0:T(8,128)} %get-tuple-element.7.stats_hbm), custom_call_target="tpu_custom_call" | custom-call | tf_op jit(solution)/shard_map/finish/pallas_call | solution.py:509

commit v4 on v3

--- a/solution.py
+++ b/solution.py
@@ -23,7 +23,8 @@
 
 GR, GL, FR, FL = (0, 1, 2, 3), (4, 5, 6, 7), (8, 9), (10, 11)
 RR, RL, D0R, D1R, D0L, D1L, WR, WL, PT = range(12, 21)
-NAMES = 21
+GR1, GL1 = 21, 22
+NAMES = 23
 
 PEERS = [(0, dz, dc) for dz in range(4) for dc in range(2) if (dz, dc) != (0, 0)] + [
     (dx, 0, dc) for dx in range(1, 4) for dc in range(2)
@@ -101,8 +102,13 @@
         i = idx(rnd, rt, kh)
         rows = pl.ds(kh * HALF + rt * Q, Q)
         if name in GR or name in GL:
-            pair = pl.ds(2 * (name % 4), 2)
+            k = name % 4
+            pair = pl.ds(2 * k, 2) if k else pl.ds(0, 1)
             d, far = (1, 2) if name in GR else (-1, 0)
+            src, dst = fld[rnd].at[pair, rows, :], gb[i].at[far, pair]
+        elif name in (GR1, GL1):
+            pair = pl.ds(1, 1)
+            d, far = (1, 2) if name == GR1 else (-1, 0)
             src, dst = fld[rnd].at[pair, rows, :], gb[i].at[far, pair]
         else:
             d, far = (1, 2) if name in FR else (-1, 0)
@@ -156,7 +162,7 @@
 
     def wait_sends(kh, rnd):
         for rt in range(2):
-            for name in GR + GL + FR + FL:
+            for name in GR + GL + FR + FL + (GR1, GL1):
                 g_copy(rnd, rt, kh, name).wait_send()
             for name in (RR, RL, D0R, D1R, D0L, D1L, WR, WL, PT):
                 p_copy(rnd, rt, kh, name).wait_send()
@@ -227,10 +233,10 @@
         hit = (seed_c[t] == column) & inside
         return BLEND * total + jnp.where(hit, jnp.float32(1.0 - BLEND), jnp.float32(0.0))
 
-    HOP = ((GR[0], GL[0]), (GR[2], GL[2]), (GR[1], GL[1]), (GR[3], GL[3]))
-    ALL_HOPS = sum(HOP, ())
-    GO_ON = (((GR[0], FR[0]), (GL[2], FL[0])), ((GR[1], FR[1]), (GL[3], FL[1])))
-    REST = (GR[2], GR[3], GL[0], GL[1]) + FR + FL
+    HOP = ((GR1, GL1), (GR[2], GL[2]), (GR[1], GL[1]), (GR[3], GL[3]))
+    ALL_HOPS = (GR[0], GL[0]) + sum(HOP, ())
+    GO_ON = (((GR1, FR[0]), (GL[2], FL[0])), ((GR[1], FR[1]), (GL[3], FL[1])))
+    REST = (GR[2], GR[3], GL[0], GL1, GL[1]) + FR + FL
     SENDS = (RR, RL, D0R, D0L, D1R, D1L, PT)
     RELAY = (WR, WL)
     FINAL = (D0R, D0L, D1R, D1L, PT, WR, WL)
@@ -241,20 +247,27 @@
     for cp in block_cps:
         cp.start()
 
-    for rnd in range(2):
-        for rt in range(2):
-            for kh in range(2):
-                cs[idx(rnd, rt, kh)][ZERO] = jnp.zeros((Q, TILE), jnp.bfloat16)
-    for t in range(TPD):
-        own_slots(0, t)
-
     def forward(rnd, kh):
+        wait_g(rnd, kh, (GR[0],))
         for part in GO_ON:
             for name, onward in part:
                 wait_g(rnd, kh, (name,))
                 start_g(rnd, kh, (onward,))
 
     def prepare():
+        for cp in f_copies:
+            cp.wait()
+        to_smem = pltpu.make_async_copy(frv, frm, loc.at[1])
+        to_smem.start()
+        to_smem.wait()
+
+    def prepare_rest():
+        for rn in range(2):
+            for rt in range(2):
+                for kh in range(2):
+                    cs[idx(rn, rt, kh)][ZERO] = jnp.zeros((Q, TILE), jnp.bfloat16)
+        for t in range(TPD):
+            own_slots(0, t)
         for cp in small_cps[1:]:
             cp.wait()
         seeds_t = jnp.transpose(seeds_ref[...].astype(jnp.float32), (1, 0))
@@ -265,10 +278,6 @@
                 half = slice(h * HALF, (h + 1) * HALF)
                 seed_r[t : t + 1, half] = seeds_ref[k : k + 1, :]
                 temp_r[t : t + 1, half] = temp_ref[k : k + 1, :]
-        for cp in f_copies:
-            cp.wait()
-        to_smem = pltpu.make_async_copy(frv, frm, loc.at[1])
-        to_smem.start()
 
         def slots(t, carry):
             count = counts_ref[t]
@@ -287,7 +296,6 @@
             return carry
 
         lax.fori_loop(0, TPD, slots, 0)
-        to_smem.wait()
 
     def exchange(rnd):
         forward(rnd, 0)
@@ -303,6 +311,8 @@
         wait_p(rnd, 0, (RR, RL))
         start_p(rnd, 0, RELAY)
         start_p(rnd, 1, SENDS)
+        if rnd == 0:
+            prepare_rest()
         wait_p(rnd, 0, FINAL)
 
     def first_chunk(rnd):
@@ -326,6 +336,10 @@
         wait_sends(kh, 0)
 
     def first_tile(i, carry):
+        @pl.when(i == 1)
+        def _():
+            start_g(1, 0, (GR[0], GL[0]))
+
         for k in range(3):
 
             @pl.when(i == 2 * k + 2)

time: 109 us -> 109 us (level)
  no operation moved by 1% of the time
where the time goes in v4:
time: 109 us
  Pallas kernels  108 us (99%)
    pallas_call x1, Pallas kernels, local(): pl.pallas_call(kernel, out_shape=(jax.ShapeDtypeStruct((TPD, TILE, TILE),...  105 us
    pallas_call x1, Pallas kernels, local(): pl.pallas_call(finish, out_shape=(jax.ShapeDtypeStruct((TPD * TILE, W), b...  3.29 us

profile of v4, /device:TPU:0, one launch (start us, length us, event | category | flops | bytes accessed | tf_op | source)
XLA Modules:
  0.0 108.8 jit_solution(926270104993017144)
XLA Ops:
  0.6 104.8 %propagate.1 = (bf16[8,256,256]{2,1,0:T(8,128)(2,1)}, f32[4,3,8,256]{3,2,1,0:T(8,128)}) custom-call(s32[8,24]{1,0:T(8,128)} %links_hbm.1, s32[8]{0:T(128)} %counts_hbm.1, s32[1,32]{1,0:T(1,128)} %bitcast.6, bf16[2048,250]{1,0:T(8,128)(2,1)} %prior_hbm.1, bf16[8,24,256,256]{3,2,1,0:T(8,128)(2,1)} %blocks_hbm.1, s32[16,128]{1,0:T(8,128)} %bitcast.4, ...), custom_call_target="tpu_custom_call" | custom-call | tf_op jit(solution)/shard_map/propagate/pallas_call | solution.py:470
  105.5 3.3 %finish.1 = (bf16[2048,250]{1,0:T(8,128)(2,1)}, f32[16,128]{1,0:T(8,128)}) custom-call(bf16[8,256,256]{2,1,0:T(8,128)(2,1)} %get-tuple-element.6.expo_hbm, f32[4,3,8,256]{3,2,1,0:T(8,128)} %get-tuple-element.7.stats_hbm), custom_call_target="tpu_custom_call" | custom-call | tf_op jit(solution)/shard_map/finish/pallas_call | solution.py:523

commit v5 on v3

--- a/solution.py
+++ b/solution.py
@@ -296,8 +296,8 @@
             prepare()
         wait_g(rnd, 0, REST)
         select(rnd, 0)
+        start_p(rnd, 0, SENDS)
         forward(rnd, 1)
-        start_p(rnd, 0, SENDS)
         wait_g(rnd, 1, REST)
         select(rnd, 1)
         wait_p(rnd, 0, (RR, RL))

time: 109 us -> 112 us (1.028)
  Pallas kernels: 108 us -> 112 us
    pallas_call x1, Pallas kernels: 104 us -> 108 us  [local(): pl.pallas_call(kernel, out_shape=(jax.ShapeDtypeStruct((TPD, TILE, TILE),...]
where the time goes in v5:
time: 112 us
  Pallas kernels  112 us (100%)
    pallas_call x1, Pallas kernels, local(): pl.pallas_call(kernel, out_shape=(jax.ShapeDtypeStruct((TPD, TILE, TILE),...  108 us
    pallas_call x1, Pallas kernels, local(): pl.pallas_call(finish, out_shape=(jax.ShapeDtypeStruct((TPD * TILE, W), b...  3.29 us

profile of v5, /device:TPU:0, one launch (start us, length us, event | category | flops | bytes accessed | tf_op | source)
XLA Modules:
  0.0 112.2 jit_solution(7969026961179778054)
XLA Ops:
  0.6 108.3 %propagate.1 = (bf16[8,256,256]{2,1,0:T(8,128)(2,1)}, f32[4,3,8,256]{3,2,1,0:T(8,128)}) custom-call(s32[8,24]{1,0:T(8,128)} %links_hbm.1, s32[8]{0:T(128)} %counts_hbm.1, s32[1,32]{1,0:T(1,128)} %bitcast.6, bf16[2048,250]{1,0:T(8,128)(2,1)} %prior_hbm.1, bf16[8,24,256,256]{3,2,1,0:T(8,128)(2,1)} %blocks_hbm.1, s32[16,128]{1,0:T(8,128)} %bitcast.4, ...), custom_call_target="tpu_custom_call" | custom-call | tf_op jit(solution)/shard_map/propagate/pallas_call | solution.py:456
  108.9 3.3 %finish.1 = (bf16[2048,250]{1,0:T(8,128)(2,1)}, f32[16,128]{1,0:T(8,128)}) custom-call(bf16[8,256,256]{2,1,0:T(8,128)(2,1)} %get-tuple-element.6.expo_hbm, f32[4,3,8,256]{3,2,1,0:T(8,128)} %get-tuple-element.7.stats_hbm), custom_call_target="tpu_custom_call" | custom-call | tf_op jit(solution)/shard_map/finish/pallas_call | solution.py:509
